TPU v7x, 32 devices: a whole 2x2x4 slice. The times are simulated.
32 devices in a mesh: section: 2 (over y), tensor: 4 (over z), dp: 4 (over x, core).
Axes of the slice: x: 2, y: 2, z: 4, core: 2. Of those that a mesh axis runs over, the one named last changes fastest.
Arguments:
- tokens_in: bfloat16 [4, 256, 4, 2048], P(None, 'tensor', 'dp'), may hold values from -6 to 6
- cotangent: bfloat16 [4, 256, 4, 2048], P(None, 'tensor', 'dp'), may hold values from -6 to 6
- ln1_gain: bfloat16 [2, 2048], P('section'), may hold values from 0.5 to 1.5
- ln1_bias: bfloat16 [2, 2048], P('section'), may hold values from -1 to 1
- q_weight: bfloat16 [2, 2048, 2048], P('section', None, 'tensor'), may hold values from -0.125 to 0.125
- q_bias: bfloat16 [2, 2048], P('section', 'tensor'), may hold values from -1.5 to 1.5
- kv_weight: bfloat16 [2, 2048, 256], P('section'), may hold values from -0.125 to 0.125
- v_bias: bfloat16 [2, 128], P('section'), may hold values from -0.25 to 0.25
- o_weight: bfloat16 [2, 2048, 2048], P('section', 'tensor'), may hold values from -1.5 to 1.5
- o_bias: bfloat16 [2, 2048], P('section'), may hold values from -1.5 to 1.5
- ln2_gain: bfloat16 [2, 2048], P('section'), may hold values from 0.5 to 1.5
- ln2_bias: bfloat16 [2, 2048], P('section'), may hold values from -1 to 1
- up_weight: bfloat16 [2, 2048, 8192], P('section', None, 'tensor'), may hold values from -0.125 to 0.125
- up_bias: bfloat16 [2, 8192], P('section', 'tensor'), may hold values from -1.5 to 1.5
- down_weight: bfloat16 [2, 8192, 2048], P('section', 'tensor'), may hold values from -0.0625 to 0.0625
- down_bias: bfloat16 [2, 2048], P('section'), may hold values from -1.5 to 1.5
Outputs:
- layer_out: bfloat16 [2, 4, 256, 4, 2048], P('section', None, 'tensor', 'dp')
- input_grad: float32 [2, 4, 256, 4, 2048], P('section', None, 'tensor', 'dp')
- ln1_gain_grad: float32 [2, 2048], P('section')
- ln1_bias_grad: float32 [2, 2048], P('section')
- q_weight_grad: float32 [2, 2048, 2048], P('section', None, 'tensor')
- q_bias_grad: float32 [2, 2048], P('section', 'tensor')
- kv_weight_grad: float32 [2, 2048, 256], P('section')
- v_bias_grad: float32 [2, 128], P('section')
- o_weight_grad: float32 [2, 2048, 2048], P('section', 'tensor')
- o_bias_grad: float32 [2, 2048], P('section')
- ln2_gain_grad: float32 [2, 2048], P('section')
- ln2_bias_grad: float32 [2, 2048], P('section')
- up_weight_grad: float32 [2, 2048, 8192], P('section', None, 'tensor')
- up_bias_grad: float32 [2, 8192], P('section', 'tensor')
- down_weight_grad: float32 [2, 8192, 2048], P('section', 'tensor')
- down_bias_grad: float32 [2, 2048], P('section')
All inputs are finite; a program needn't handle non-finite values.
Results may differ from a plain program's by a relative error of at most 0.022.
Values may be sent and summed in bfloat16 or wider, within the bound.
A program may use at most 512 MiB of HBM per device.

v0:
```python
import math
import jax
import jax.numpy as jnp
from jax import lax
from jax.sharding import PartitionSpec as P

HD = 128


def from_behind(block, axis, distance):
    devices = range(lax.axis_size(axis))
    route = [(i - distance, i) for i in devices if i - distance in devices]
    return lax.ppermute(block, axis, route)


def for_sending(shard):
    return jax.tree.map(lambda a: a.astype(jnp.bfloat16) if a.dtype == jnp.float32 else a, shard)


def layer_norm(values, gain_vec, bias_vec):
    row_mean = jnp.mean(values, axis=-1, keepdims=True)
    centred = values - row_mean
    row_var = jnp.mean(centred * centred, axis=-1, keepdims=True)
    return centred * lax.rsqrt(row_var + 1e-05) * gain_vec + bias_vec


def gelu_tanh(values):
    return jax.nn.gelu(values, approximate=True)


def gather_rows(own_rows):
    return lax.all_gather(own_rows, "tensor", axis=0, tiled=True)


def sum_rows(term_fn, own_count):
    return lax.psum_scatter(
        term_fn(jnp.int32(0), own_count * lax.axis_size("tensor")).astype(jnp.bfloat16),
        "tensor",
        scatter_dimension=0,
        tiled=True,
    ).astype(jnp.float32)


def on_device(
    tokens_in,
    cotangent,
    ln1_gain,
    ln1_bias,
    q_weight,
    q_bias,
    kv_weight,
    v_bias,
    o_weight,
    o_bias,
    ln2_gain,
    ln2_bias,
    up_weight,
    up_bias,
    down_weight,
    down_bias,
):
    f32 = jnp.float32
    bf16 = jnp.bfloat16
    section = lax.axis_index("section")
    tensor_count = lax.axis_size("tensor")
    tensor_rank = lax.axis_index("tensor")
    gain_one = ln1_gain[0].astype(f32)
    bias_one = ln1_bias[0].astype(f32)
    w_query = q_weight[0]
    b_query = q_bias[0].astype(f32)
    w_pairs = kv_weight[0]
    pair_bias = jnp.concatenate([jnp.zeros((HD,), f32), v_bias[0].astype(f32)])
    w_out = o_weight[0]
    b_out = o_bias[0].astype(f32)
    gain_two = ln2_gain[0].astype(f32)
    bias_two = ln2_bias[0].astype(f32)
    w_up = up_weight[0]
    b_up = up_bias[0].astype(f32)
    w_down = down_weight[0]
    b_down = down_bias[0].astype(f32)
    blocks, own_count, seq_count, model_dim = tokens_in.shape
    block_len = own_count * tensor_count
    total_len = blocks * block_len
    heads_local = w_query.shape[1] // HD
    ff_local = w_up.shape[1]
    score_scale = 1.0 / math.sqrt(HD)
    positions = jnp.arange(total_len, dtype=jnp.int32)
    own_start = tensor_rank * own_count
    kept_normed = jnp.zeros((blocks, block_len, seq_count, model_dim), bf16)
    kept_query = jnp.zeros((blocks, block_len, seq_count, heads_local * HD), bf16)
    kept_attended = jnp.zeros((blocks, block_len, seq_count, heads_local * HD), bf16)
    kept_logsum = jnp.zeros((blocks, seq_count, block_len, heads_local), f32)
    kv_cache = jnp.zeros((total_len, seq_count, 2 * HD), bf16)
    kept_input = jnp.zeros((blocks, own_count, seq_count, model_dim), f32)
    kept_hidden = jnp.zeros((blocks, own_count, seq_count, model_dim), f32)
    kept_normed_two = jnp.zeros((blocks, block_len, seq_count, model_dim), bf16)
    kept_pre = jnp.zeros((blocks, block_len, seq_count, ff_local), f32)
    outputs = jnp.zeros((blocks, own_count, seq_count, model_dim), bf16)
    received = jnp.zeros((own_count, seq_count, model_dim), f32)
    for turn in range(blocks + 1):
        block_index = jnp.clip(turn - section, 0, blocks - 1)
        from_input = lax.dynamic_index_in_dim(tokens_in, block_index, 0, keepdims=False).astype(f32)
        layer_input = jnp.where(section == 0, from_input, received)
        normed = gather_rows(layer_norm(layer_input, gain_one, bias_one).astype(bf16))
        query = (
            jnp.einsum("rsd,de->rse", normed, w_query, preferred_element_type=f32) + b_query
        ).astype(bf16)
        pairs = jnp.einsum("rsd,dc->rsc", normed, w_pairs, preferred_element_type=f32) + pair_bias
        kv_cache = lax.dynamic_update_slice_in_dim(
            kv_cache, pairs.astype(bf16), block_index * block_len, 0
        )
        key_rows = kv_cache[..., :HD]
        value_rows = kv_cache[..., HD:]
        visible = positions < (block_index + 1) * block_len
        query_heads = query.reshape(block_len, seq_count, heads_local, HD)
        scores = (
            jnp.einsum("qshd,ksd->sqhk", query_heads, key_rows, preferred_element_type=f32)
            * score_scale
        )
        scores = jnp.where(visible, scores, -1e30)
        row_top = jnp.max(scores, axis=-1, keepdims=True)
        exponent = jnp.exp(scores - row_top)
        row_total = jnp.sum(exponent, axis=-1, keepdims=True)
        log_total = (row_top + jnp.log(row_total))[..., 0]
        weights_low = (exponent / row_total).astype(bf16)
        attended = jnp.einsum("sqhk,ksd->qshd", weights_low, value_rows, preferred_element_type=f32)
        attended = attended.reshape(block_len, seq_count, heads_local * HD).astype(bf16)

        def attention_term(start, count, attended=attended):
            return jnp.einsum("rse,ed->rsd", attended, w_out, preferred_element_type=f32)

        hidden = layer_input + sum_rows(attention_term, own_count) + b_out
        normed_two = gather_rows(layer_norm(hidden, gain_two, bias_two).astype(bf16))
        pre_active = jnp.einsum("rsd,df->rsf", normed_two, w_up, preferred_element_type=f32) + b_up
        active = gelu_tanh(pre_active).astype(bf16)

        def feed_term(start, count, active=active):
            return jnp.einsum("rsf,fd->rsd", active, w_down, preferred_element_type=f32)

        result_low = (hidden + sum_rows(feed_term, own_count) + b_down).astype(bf16)
        kept_normed = lax.dynamic_update_index_in_dim(kept_normed, normed, block_index, 0)
        kept_query = lax.dynamic_update_index_in_dim(kept_query, query, block_index, 0)
        kept_attended = lax.dynamic_update_index_in_dim(kept_attended, attended, block_index, 0)
        kept_logsum = lax.dynamic_update_index_in_dim(kept_logsum, log_total, block_index, 0)
        kept_input = lax.dynamic_update_index_in_dim(kept_input, layer_input, block_index, 0)
        kept_hidden = lax.dynamic_update_index_in_dim(kept_hidden, hidden, block_index, 0)
        kept_normed_two = lax.dynamic_update_index_in_dim(
            kept_normed_two, normed_two, block_index, 0
        )
        kept_pre = lax.dynamic_update_index_in_dim(kept_pre, pre_active, block_index, 0)
        outputs = lax.dynamic_update_index_in_dim(outputs, result_low, block_index, 0)
        received = from_behind(result_low, "section", 1).astype(f32)
    key_rows = kv_cache[..., :HD]
    value_rows = kv_cache[..., HD:]
    sharded_total = (
        jnp.zeros(w_query.shape, f32),
        jnp.zeros(b_query.shape, f32),
        jnp.zeros(w_out.shape, f32),
        jnp.zeros(w_up.shape, f32),
        jnp.zeros(b_up.shape, f32),
        jnp.zeros(w_down.shape, f32),
    )
    common_total = (
        jnp.zeros(gain_one.shape, f32),
        jnp.zeros(bias_one.shape, f32),
        jnp.zeros(b_out.shape, f32),
        jnp.zeros(gain_two.shape, f32),
        jnp.zeros(bias_two.shape, f32),
        jnp.zeros(b_down.shape, f32),
    )
    pair_total = (jnp.zeros(w_pairs.shape, f32), jnp.zeros((HD,), f32))
    sharded_total = sharded_total + pair_total
    pair_grad_acc = jnp.zeros((total_len, seq_count, 2 * HD), f32)
    input_grads = jnp.zeros((blocks, own_count, seq_count, model_dim), f32)
    received_back = jnp.zeros((own_count, seq_count, model_dim), f32)
    for turn in range(blocks + 1):
        step_count = turn - (1 - section)
        valid = (step_count >= 0) & (step_count < blocks)
        valid_scale = valid.astype(f32)
        block_index = blocks - 1 - jnp.clip(step_count, 0, blocks - 1)
        from_cot = lax.dynamic_index_in_dim(cotangent, block_index, 0, keepdims=False).astype(f32)
        grad_out = jnp.where(section == 1, from_cot, received_back) * valid_scale
        pre_active = lax.dynamic_index_in_dim(kept_pre, block_index, 0, keepdims=False)
        normed_two = lax.dynamic_index_in_dim(kept_normed_two, block_index, 0, keepdims=False)
        active = gelu_tanh(pre_active).astype(bf16)
        grad_mlp = gather_rows(grad_out.astype(bf16))
        grad_active = jnp.einsum("rsd,fd->rsf", grad_mlp, w_down, preferred_element_type=f32)
        gelu_back = jax.vjp(gelu_tanh, pre_active)[1]
        grad_pre = gelu_back(grad_active)[0].astype(bf16)
        down_w_term = jnp.einsum("rsf,rsd->fd", active, grad_mlp, preferred_element_type=f32)
        up_w_term = jnp.einsum("rsd,rsf->df", normed_two, grad_pre, preferred_element_type=f32)
        up_b_term = jnp.sum(grad_pre.astype(f32), axis=(0, 1))
        down_b_term = jnp.sum(grad_out, axis=(0, 1))

        def feed_back_term(start, count, grad_pre=grad_pre):
            return jnp.einsum("rsf,df->rsd", grad_pre, w_up, preferred_element_type=f32)

        grad_normed_two = sum_rows(feed_back_term, own_count)
        hidden_own = lax.dynamic_index_in_dim(kept_hidden, block_index, 0, keepdims=False)
        norm_back_two = jax.vjp(layer_norm, hidden_own, gain_two, bias_two)[1]
        grad_hidden_norm, gain_two_term, bias_two_term = norm_back_two(grad_normed_two)
        grad_hidden = grad_out + grad_hidden_norm
        out_b_term = jnp.sum(grad_hidden, axis=(0, 1))
        grad_branch = gather_rows(grad_hidden.astype(bf16))
        attended = lax.dynamic_index_in_dim(kept_attended, block_index, 0, keepdims=False)
        out_w_term = jnp.einsum("rse,rsd->ed", attended, grad_branch, preferred_element_type=f32)
        grad_attended = jnp.einsum(
            "rsd,ed->rse", grad_branch, w_out, preferred_element_type=f32
        ).astype(bf16)
        grad_attended = grad_attended.reshape(block_len, seq_count, heads_local, HD)
        query = lax.dynamic_index_in_dim(kept_query, block_index, 0, keepdims=False)
        query_heads = query.reshape(block_len, seq_count, heads_local, HD)
        log_total = lax.dynamic_index_in_dim(kept_logsum, block_index, 0, keepdims=False)
        visible = positions < (block_index + 1) * block_len
        scores = (
            jnp.einsum("qshd,ksd->sqhk", query_heads, key_rows, preferred_element_type=f32)
            * score_scale
        )
        scores = jnp.where(visible, scores, -1e30)
        probabilities = jnp.exp(scores - log_total[..., None])
        grad_probs = jnp.einsum(
            "qshd,ksd->sqhk", grad_attended, value_rows, preferred_element_type=f32
        )
        row_inner = jnp.sum(probabilities * grad_probs, axis=-1, keepdims=True)
        grad_scores = (probabilities * (grad_probs - row_inner)).astype(bf16)
        grad_query = (
            jnp.einsum("sqhk,ksd->qshd", grad_scores, key_rows, preferred_element_type=f32)
            * score_scale
        )
        grad_query = grad_query.astype(bf16).reshape(block_len, seq_count, heads_local * HD)
        grad_keys = (
            jnp.einsum("sqhk,qshd->ksd", grad_scores, query_heads, preferred_element_type=f32)
            * score_scale
        )
        grad_values = jnp.einsum(
            "sqhk,qshd->ksd", probabilities.astype(bf16), grad_attended, preferred_element_type=f32
        )
        pair_grad_acc = pair_grad_acc + jnp.concatenate([grad_keys, grad_values], axis=-1)
        block_pairs = lax.dynamic_slice_in_dim(pair_grad_acc, block_index * block_len, block_len, 0)
        grad_pairs = (
            lax.psum(block_pairs.astype(jnp.bfloat16), "tensor").astype(jnp.float32) * valid_scale
        ).astype(bf16)
        normed = lax.dynamic_index_in_dim(kept_normed, block_index, 0, keepdims=False)
        query_w_term = jnp.einsum("rsd,rse->de", normed, grad_query, preferred_element_type=f32)
        query_b_term = jnp.sum(grad_query.astype(f32), axis=(0, 1))
        own_pairs = lax.dynamic_slice_in_dim(grad_pairs, own_start, own_count, 0)
        pair_w_term = jnp.einsum("rsd,rsc->dc", normed, grad_pairs, preferred_element_type=f32)
        value_b_term = jnp.sum(grad_pairs[..., HD:].astype(f32), axis=(0, 1))

        def attention_back_term(start, count, grad_query=grad_query):
            return jnp.einsum("rse,de->rsd", grad_query, w_query, preferred_element_type=f32)

        grad_normed = sum_rows(attention_back_term, own_count)
        grad_normed = grad_normed + jnp.einsum(
            "rsc,dc->rsd", own_pairs, w_pairs, preferred_element_type=f32
        )
        layer_input = lax.dynamic_index_in_dim(kept_input, block_index, 0, keepdims=False)
        norm_back_one = jax.vjp(layer_norm, layer_input, gain_one, bias_one)[1]
        grad_input_norm, gain_one_term, bias_one_term = norm_back_one(grad_normed)
        grad_input = grad_hidden + grad_input_norm
        previous = lax.dynamic_index_in_dim(input_grads, block_index, 0, keepdims=False)
        input_grads = lax.dynamic_update_index_in_dim(
            input_grads, jnp.where(valid, grad_input, previous), block_index, 0
        )
        received_back = from_behind(grad_input.astype(jnp.bfloat16), "section", -1).astype(
            grad_input.dtype
        )
        sharded_terms = (query_w_term, query_b_term, out_w_term, up_w_term, up_b_term, down_w_term)
        common_terms = (
            gain_one_term,
            bias_one_term,
            out_b_term,
            gain_two_term,
            bias_two_term,
            down_b_term,
        )
        pair_terms = (pair_w_term, value_b_term)
        sharded_terms = sharded_terms + pair_terms
        sharded_total = jax.tree.map(jnp.add, sharded_total, sharded_terms)
        common_total = jax.tree.map(jnp.add, common_total, common_terms)
    sharded_total = jax.tree.map(
        lambda part: part.astype(jnp.float32), lax.psum(for_sending(sharded_total), "dp")
    )
    common_total = lax.psum(common_total, ("tensor", "dp"))
    pair_w_grad, value_b_grad = (sharded_total[6], sharded_total[7])
    return (
        outputs[None],
        input_grads[None],
        common_total[0][None],
        common_total[1][None],
        sharded_total[0][None],
        sharded_total[1][None],
        pair_w_grad[None],
        value_b_grad[None],
        sharded_total[2][None],
        common_total[2][None],
        common_total[3][None],
        common_total[4][None],
        sharded_total[3][None],
        sharded_total[4][None],
        sharded_total[5][None],
        common_total[5][None],
    )


def solution(mesh):
    placed = (
        P(None, "tensor", "dp", None),
        P(None, "tensor", "dp", None),
        P("section", None),
        P("section", None),
        P("section", None, "tensor"),
        P("section", "tensor"),
        P("section", None, None),
        P("section", None),
        P("section", "tensor", None),
        P("section", None),
        P("section", None),
        P("section", None),
        P("section", None, "tensor"),
        P("section", "tensor"),
        P("section", "tensor", None),
        P("section", None),
    )
    return jax.shard_map(
        on_device,
        mesh=mesh,
        in_specs=placed,
        out_specs=(
            P("section", None, "tensor", "dp", None),
            P("section", None, "tensor", "dp", None),
            P("section", None),
            P("section", None),
            P("section", None, "tensor"),
            P("section", "tensor"),
            P("section", None, None),
            P("section", None),
            P("section", "tensor", None),
            P("section", None),
            P("section", None),
            P("section", None),
            P("section", None, "tensor"),
            P("section", "tensor"),
            P("section", "tensor", None),
            P("section", None),
        ),
        check_vma=False,
    )
```

profile of v0, /device:TPU:0, one launch (start us, length us, event | category | flops | bytes accessed | tf_op | source)
XLA Modules:
  0.0 2236.9 jit_solution(8627879829273172787)
XLA Ops:
  15.2 29.4 %all-gather.21.cloned.1.call-done = bf16[256,1,2048]{2,0,1:T(8,128)(2,1)} async-done(((bf16[64,1,2048]{2,0,1:T(8,128)(2,1)}), bf16[256,1,2048]{2,0,1:T(8,128)(2,1)}) %all-gather.21.cloned.1.call-update) | async-done | bytes 1048592 | tf_op jit(solution)/shard_map/all_gather | solution.py:32
  53.2 26.7 %reduce-scatter.21.cloned.1.call-done = bf16[64,1,2048]{2,0,1:T(8,128)(2,1)} async-done(((bf16[256,1,2048]{2,0,1:T(8,128)(2,1)}), bf16[64,1,2048]{2,0,1:T(8,128)(2,1)}) %reduce-scatter.21.cloned.1.call-update) | async-done | bytes 262160 | tf_op jit(solution)/shard_map/reduce_scatter | solution.py:36
  85.2 26.6 %all-gather.23.cloned.1.call-done = bf16[256,1,2048]{2,0,1:T(8,128)(2,1)} async-done(((bf16[64,1,2048]{2,0,1:T(8,128)(2,1)}), bf16[256,1,2048]{2,0,1:T(8,128)(2,1)}) %all-gather.23.cloned.1.call-update) | async-done | bytes 1048592 | tf_op jit(solution)/shard_map/all_gather | solution.py:32
  127.1 26.7 %reduce-scatter.23.cloned.1.call-done = bf16[64,1,2048]{2,0,1:T(8,128)(2,1)} async-done(((bf16[256,1,2048]{2,0,1:T(8,128)(2,1)}), bf16[64,1,2048]{2,0,1:T(8,128)(2,1)}) %reduce-scatter.23.cloned.1.call-update) | async-done | bytes 262160 | tf_op jit(solution)/shard_map/reduce_scatter | solution.py:36
  170.1 27.7 %all-gather.25.cloned.1.call-done = bf16[256,1,2048]{2,0,1:T(8,128)(2,1)} async-done(((bf16[64,1,2048]{2,0,1:T(8,128)(2,1)}), bf16[256,1,2048]{2,0,1:T(8,128)(2,1)}) %all-gather.25.cloned.1.call-update) | async-done | bytes 1048592 | tf_op jit(solution)/shard_map/all_gather | solution.py:32
  206.2 26.7 %reduce-scatter.25.cloned.1.call-done = bf16[64,1,2048]{2,0,1:T(8,128)(2,1)} async-done(((bf16[256,1,2048]{2,0,1:T(8,128)(2,1)}), bf16[64,1,2048]{2,0,1:T(8,128)(2,1)}) %reduce-scatter.25.cloned.1.call-update) | async-done | bytes 262160 | tf_op jit(solution)/shard_map/reduce_scatter | solution.py:36
  235.4 26.7 %all-gather.27.cloned.1.call-done = bf16[256,1,2048]{2,0,1:T(8,128)(2,1)} async-done(((bf16[64,1,2048]{2,0,1:T(8,128)(2,1)}), bf16[256,1,2048]{2,0,1:T(8,128)(2,1)}) %all-gather.27.cloned.1.call-update) | async-done | bytes 1048592 | tf_op jit(solution)/shard_map/all_gather | solution.py:32
  276.4 26.8 %reduce-scatter.27.cloned.1.call-done = bf16[64,1,2048]{2,0,1:T(8,128)(2,1)} async-done(((bf16[256,1,2048]{2,0,1:T(8,128)(2,1)}), bf16[64,1,2048]{2,0,1:T(8,128)(2,1)}) %reduce-scatter.27.cloned.1.call-update) | async-done | bytes 262160 | tf_op jit(solution)/shard_map/reduce_scatter | solution.py:36
  319.5 27.4 %all-gather.29.cloned.1.call-done = bf16[256,1,2048]{2,0,1:T(8,128)(2,1)} async-done(((bf16[64,1,2048]{2,0,1:T(8,128)(2,1)}), bf16[256,1,2048]{2,0,1:T(8,128)(2,1)}) %all-gather.29.cloned.1.call-update) | async-done | bytes 1048592 | tf_op jit(solution)/shard_map/all_gather | solution.py:32
  355.9 26.7 %reduce-scatter.29.cloned.1.call-done = bf16[64,1,2048]{2,0,1:T(8,128)(2,1)} async-done(((bf16[256,1,2048]{2,0,1:T(8,128)(2,1)}), bf16[64,1,2048]{2,0,1:T(8,128)(2,1)}) %reduce-scatter.29.cloned.1.call-update) | async-done | bytes 262160 | tf_op jit(solution)/shard_map/reduce_scatter | solution.py:36
  385.7 26.7 %all-gather.31.cloned.1.call-done = bf16[256,1,2048]{2,0,1:T(8,128)(2,1)} async-done(((bf16[64,1,2048]{2,0,1:T(8,128)(2,1)}), bf16[256,1,2048]{2,0,1:T(8,128)(2,1)}) %all-gather.31.cloned.1.call-update) | async-done | bytes 1048592 | tf_op jit(solution)/shard_map/all_gather | solution.py:32
  426.7 26.7 %reduce-scatter.31.cloned.1.call-done = bf16[64,1,2048]{2,0,1:T(8,128)(2,1)} async-done(((bf16[256,1,2048]{2,0,1:T(8,128)(2,1)}), bf16[64,1,2048]{2,0,1:T(8,128)(2,1)}) %reduce-scatter.31.cloned.1.call-update) | async-done | bytes 262160 | tf_op jit(solution)/shard_map/reduce_scatter | solution.py:36
  469.6 27.6 %all-gather.33.cloned.1.call-done = bf16[256,1,2048]{2,0,1:T(8,128)(2,1)} async-done(((bf16[64,1,2048]{2,0,1:T(8,128)(2,1)}), bf16[256,1,2048]{2,0,1:T(8,128)(2,1)}) %all-gather.33.cloned.1.call-update) | async-done | bytes 1048592 | tf_op jit(solution)/shard_map/all_gather | solution.py:32
  506.4 26.7 %reduce-scatter.33.cloned.1.call-done = bf16[64,1,2048]{2,0,1:T(8,128)(2,1)} async-done(((bf16[256,1,2048]{2,0,1:T(8,128)(2,1)}), bf16[64,1,2048]{2,0,1:T(8,128)(2,1)}) %reduce-scatter.33.cloned.1.call-update) | async-done | bytes 262160 | tf_op jit(solution)/shard_map/reduce_scatter | solution.py:36
  536.1 26.7 %all-gather.35.cloned.1.call-done = bf16[256,1,2048]{2,0,1:T(8,128)(2,1)} async-done(((bf16[64,1,2048]{2,0,1:T(8,128)(2,1)}), bf16[256,1,2048]{2,0,1:T(8,128)(2,1)}) %all-gather.35.cloned.1.call-update) | async-done | bytes 1048592 | tf_op jit(solution)/shard_map/all_gather | solution.py:32
  577.1 26.8 %reduce-scatter.35.cloned.1.call-done = bf16[64,1,2048]{2,0,1:T(8,128)(2,1)} async-done(((bf16[256,1,2048]{2,0,1:T(8,128)(2,1)}), bf16[64,1,2048]{2,0,1:T(8,128)(2,1)}) %reduce-scatter.35.cloned.1.call-update) | async-done | bytes 262160 | tf_op jit(solution)/shard_map/reduce_scatter | solution.py:36
  620.0 27.8 %all-gather.37.cloned.1.call-done = bf16[256,1,2048]{2,0,1:T(8,128)(2,1)} async-done(((bf16[64,1,2048]{2,0,1:T(8,128)(2,1)}), bf16[256,1,2048]{2,0,1:T(8,128)(2,1)}) %all-gather.37.cloned.1.call-update) | async-done | bytes 1048592 | tf_op jit(solution)/shard_map/all_gather | solution.py:32
  656.9 26.7 %reduce-scatter.37.cloned.1.call-done = bf16[64,1,2048]{2,0,1:T(8,128)(2,1)} async-done(((bf16[256,1,2048]{2,0,1:T(8,128)(2,1)}), bf16[64,1,2048]{2,0,1:T(8,128)(2,1)}) %reduce-scatter.37.cloned.1.call-update) | async-done | bytes 262160 | tf_op jit(solution)/shard_map/reduce_scatter | solution.py:36
  721.4 20.9 all-gather.41.cloned.1.call-done
  742.3 8.4 convert_reduce_fusion.4
  772.6 12.6 reduce-scatter.41.cloned.1.call-done
  804.9 15.0 all-gather.43.cloned.1.call-done
  850.9 16.6 all-reduce.11.cloned.1.call-done
  868.4 28.7 %reduce-scatter.43.cloned.1.call-done = bf16[64,1,2048]{2,0,1:T(8,128)(2,1)} async-done(((bf16[256,1,2048]{2,0,1:T(8,128)(2,1)}), bf16[64,1,2048]{2,0,1:T(8,128)(2,1)}) %reduce-scatter.43.cloned.1.call-update) | async-done | bytes 262160 | tf_op jit(solution)/shard_map/reduce_scatter | solution.py:36
  902.6 8.8 collective-permute-done.4
  913.3 26.0 %all-gather.45.cloned.1.call-done = bf16[256,1,2048]{2,0,1:T(8,128)(2,1)} async-done(((bf16[64,1,2048]{2,0,1:T(8,128)(2,1)}), bf16[256,1,2048]{2,0,1:T(8,128)(2,1)}) %all-gather.45.cloned.1.call-update) | async-done | bytes 1048592 | tf_op jit(solution)/shard_map/all_gather | solution.py:32
  939.3 8.4 convert_reduce_fusion.3
  956.6 25.6 %reduce-scatter.45.cloned.1.call-done = bf16[64,1,2048]{2,0,1:T(8,128)(2,1)} async-done(((bf16[256,1,2048]{2,0,1:T(8,128)(2,1)}), bf16[64,1,2048]{2,0,1:T(8,128)(2,1)}) %reduce-scatter.45.cloned.1.call-update) | async-done | bytes 262160 | tf_op jit(solution)/shard_map/reduce_scatter | solution.py:36
  995.0 22.0 all-gather.47.cloned.1.call-done
  1045.5 20.9 all-reduce.13.cloned.1.call-done
  1067.9 28.1 %reduce-scatter.47.cloned.1.call-done = bf16[64,1,2048]{2,0,1:T(8,128)(2,1)} async-done(((bf16[256,1,2048]{2,0,1:T(8,128)(2,1)}), bf16[64,1,2048]{2,0,1:T(8,128)(2,1)}) %reduce-scatter.47.cloned.1.call-update) | async-done | bytes 262160 | tf_op jit(solution)/shard_map/reduce_scatter | solution.py:36
  1101.7 8.8 collective-permute-done.5
  1112.6 25.8 %all-gather.49.cloned.1.call-done = bf16[256,1,2048]{2,0,1:T(8,128)(2,1)} async-done(((bf16[64,1,2048]{2,0,1:T(8,128)(2,1)}), bf16[256,1,2048]{2,0,1:T(8,128)(2,1)}) %all-gather.49.cloned.1.call-update) | async-done | bytes 1048592 | tf_op jit(solution)/shard_map/all_gather | solution.py:32
  1138.4 8.4 convert_reduce_fusion.2
  1155.6 25.7 %reduce-scatter.49.cloned.1.call-done = bf16[64,1,2048]{2,0,1:T(8,128)(2,1)} async-done(((bf16[256,1,2048]{2,0,1:T(8,128)(2,1)}), bf16[64,1,2048]{2,0,1:T(8,128)(2,1)}) %reduce-scatter.49.cloned.1.call-update) | async-done | bytes 262160 | tf_op jit(solution)/shard_map/reduce_scatter | solution.py:36
  1193.8 22.2 all-gather.51.cloned.1.call-done
  1242.7 22.7 %all-reduce.15.cloned.1.call-done = bf16[256,1,256]{0,2,1:T(8,128)(2,1)} async-done(((bf16[256,1,256]{0,2,1:T(8,128)(2,1)}), bf16[256,1,256]{0,2,1:T(8,128)(2,1)}) %all-reduce.15.cloned.1.call-update) | async-done | bytes 131088 | tf_op jit(solution)/shard_map/psum | solution.py:241
  1266.9 28.2 %reduce-scatter.51.cloned.1.call-done = bf16[64,1,2048]{2,0,1:T(8,128)(2,1)} async-done(((bf16[256,1,2048]{2,0,1:T(8,128)(2,1)}), bf16[64,1,2048]{2,0,1:T(8,128)(2,1)}) %reduce-scatter.51.cloned.1.call-update) | async-done | bytes 262160 | tf_op jit(solution)/shard_map/reduce_scatter | solution.py:36
  1300.8 8.8 collective-permute-done.6
  1311.7 25.7 %all-gather.53.cloned.1.call-done = bf16[256,1,2048]{2,0,1:T(8,128)(2,1)} async-done(((bf16[64,1,2048]{2,0,1:T(8,128)(2,1)}), bf16[256,1,2048]{2,0,1:T(8,128)(2,1)}) %all-gather.53.cloned.1.call-update) | async-done | bytes 1048592 | tf_op jit(solution)/shard_map/all_gather | solution.py:32
  1337.5 8.3 convert_reduce_fusion.1
  1354.7 25.6 %reduce-scatter.53.cloned.1.call-done = bf16[64,1,2048]{2,0,1:T(8,128)(2,1)} async-done(((bf16[256,1,2048]{2,0,1:T(8,128)(2,1)}), bf16[64,1,2048]{2,0,1:T(8,128)(2,1)}) %reduce-scatter.53.cloned.1.call-update) | async-done | bytes 262160 | tf_op jit(solution)/shard_map/reduce_scatter | solution.py:36
  1393.8 21.3 all-gather.55.cloned.1.call-done
  1444.5 20.0 all-reduce.17.cloned.1.call-done
  1466.0 28.0 %reduce-scatter.55.cloned.1.call-done = bf16[64,1,2048]{2,0,1:T(8,128)(2,1)} async-done(((bf16[256,1,2048]{2,0,1:T(8,128)(2,1)}), bf16[64,1,2048]{2,0,1:T(8,128)(2,1)}) %reduce-scatter.55.cloned.1.call-update) | async-done | bytes 262160 | tf_op jit(solution)/shard_map/reduce_scatter | solution.py:36
  1516.6 20.5 all-gather.57.cloned.1.call-done
  1537.1 8.3 convert_reduce_fusion
  1561.3 18.7 reduce-scatter.57.cloned.1.call-done
  1600.7 13.6 all-gather.59.cloned.1.call-done
  1626.3 9.7 fusion.453
  1636.4 10.2 fusion.444
  1656.2 9.4 fusion.451
  1665.6 10.0 fusion.442
  1685.1 10.1 fusion.449
  1695.2 10.1 fusion.440
  1714.8 9.9 fusion.447
  1724.7 10.0 fusion.438
  1745.7 26.9 %fusion.41 = bf16[1,2048,2048]{2,1,0:T(8,128)(2,1)} fusion(f32[2048,2048]{1,0:T(8,128)} %fusion.438, f32[2048,2048]{1,0:T(8,128)} %fusion.440, f32[2048,2048]{1,0:T(8,128)} %fusion.444, f32[2048,2048]{1,0:T(8,128)} %fusion.442, bf16[256,1,2048]{2,0,1:T(8,128)(2,1)S(1)} %copy-done.77, f32[4,256,1,2048]{3,1,2,0:T(8,128)} %get-tuple-element.207, s32[]{:T(128)S(6)} %select_n.364), kind=kOutput, calls=%fused_computation.43 | convolution fusion | flops 2173173760 | bytes 78643200 | tf_op jit(solution)/shard_map/rsf,rsd->fd/dot_general | solution.py:190
  1776.0 27.2 %fusion.40 = bf16[1,2048,2048]{2,1,0:T(8,128)(2,1)} fusion(bf16[256,2048]{1,0:T(8,128)(2,1)} %copy-done.78, f32[2048,2048]{1,0:T(8,128)} %fusion.447, f32[2048,2048]{1,0:T(8,128)} %fusion.449, f32[2048,2048]{1,0:T(8,128)} %fusion.453, f32[2048,2048]{1,0:T(8,128)} %fusion.451, bf16[4,256,1,2048]{3,1,2,0:T(8,128)(2,1)} %bitcast_dynamic-update-slice_fusion.5, ...), kind=kOutput, calls=%fused_computation.42 | convolution fusion | flops 2168455168 | bytes 77594624 | tf_op jit(solution)/shard_map/rsd,rsf->df/dot_general | solution.py:191
  1834.4 11.7 all-reduce.2
  1850.6 61.3 %all-reduce.1 = (f32[1,2048]{1,0:T(1,128)}, f32[1,2048]{1,0:T(1,128)}, f32[1,2048]{1,0:T(1,128)}, f32[1,2048]{1,0:T(1,128)}, f32[1,2048]{1,0:T(1,128)}, /*index=5*/f32[1,2048]{1,0:T(1,128)}) all-reduce(f32[1,2048]{1,0:T(1,128)S(1)} %bitcast.1391, ...), channel_id=1, replica_groups=mesh['section'=2,'tensor'=4,'dp'=4] {'tensor','dp'}, use_global_device_ids=true, to_apply=%region_105.106 | all-reduce | flops 12288 | bytes 98304 | tf_op jit(solution)/shard_map/psum | solution.py:284
  1916.2 281.2 %all-reduce.21.cloned.1.call-done = (bf16[1,2048,512]{2,1,0:T(8,128)(2,1)}, bf16[1,2048,256]{2,1,0:T(8,128)(2,1)}, bf16[1,512,2048]{2,1,0:T(8,128)(2,1)}, bf16[1...) async-done(((bf16[1,2048,512]{2,1,0:T(8,128)(2,1)}, bf16[1,2048,256]{2,1,0:T(8,128)(2,1)}, bf16[1,512,2048]{2,1,0:T(8,128)(2,1)}, bf16[1,2048,2048]{2,1,0:T(8,128)(2,1)}, ...) | async-done | bytes 22020112 | tf_op jit(solution)/shard_map/psum | solution.py:282
  2206.6 11.7 broadcast_in_dim.547
  2218.2 11.7 broadcast_in_dim.551
  (897 shorter events, 639.0 us)
Async XLA Ops:
  7.2 44.1 %copy-start = (bf16[1,512,2048]{2,1,0:T(8,128)(2,1)S(1)}, bf16[1,512,2048]{2,1,0:T(8,128)(2,1)}, u32[]{:S(2)}) copy-start(bf16[1,512,2048]{2,1,0:T(8,128)(2,1)} %param.24) | copy-start | bytes 6291460
  7.2 37.4 %all-gather.21.cloned.1.call-start = ((), (), s32[]{:S(2)}) async-start(), calls=%async_computation.20 | async-start | bytes 1310720 | tf_op jit(solution)/shard_map/all_gather | solution.py:32
  8.8 1488.0 %copy-start.56 = (f32[1,2048]{1,0:T(1,128)}, f32[1,2048]{1,0:T(1,128)S(1)}, u32[]{:S(2)}) copy-start(f32[1,2048]{1,0:T(1,128)S(1)} %convert_element_type.1359) | copy-start | bytes 24580
  13.8 66.1 %reduce-scatter.21.cloned.1.call-start = ((), (), s32[]{:S(2)}) async-start(), calls=%async_computation.21 | async-start | bytes 1310720 | tf_op jit(solution)/shard_map/reduce_scatter | solution.py:36
  53.0 32.2 %copy-start.169 = (bf16[1,2048]{1,0:T(2,128)(2,1)S(1)}, bf16[1,2048]{1,0:T(2,128)(2,1)}, u32[]{:S(2)}) copy-start(bf16[1,2048]{1,0:T(2,128)(2,1)} %param.29) | copy-start | bytes 12292
  53.1 58.8 %all-gather.23.cloned.1.call-start = ((), (), s32[]{:S(2)}) async-start(), calls=%async_computation.22 | async-start | bytes 1310720 | tf_op jit(solution)/shard_map/all_gather | solution.py:32
  85.1 68.7 %reduce-scatter.23.cloned.1.call-start = ((), (), s32[]{:S(2)}) async-start(), calls=%async_computation.23 | async-start | bytes 1310720 | tf_op jit(solution)/shard_map/reduce_scatter | solution.py:36
  127.1 70.7 %all-gather.25.cloned.1.call-start = ((), (), s32[]{:S(2)}) async-start(), calls=%async_computation.24 | async-start | bytes 1310720 | tf_op jit(solution)/shard_map/all_gather | solution.py:32
  127.1 476.8 %copy-start.132 = (f32[1,2048]{1,0:T(1,128)}, f32[1,2048]{1,0:T(1,128)S(1)}, u32[]{:S(2)}) copy-start(f32[1,2048]{1,0:T(1,128)S(1)} %convert_element_type.1366) | copy-start | bytes 24580
  156.1 8.8 collective-permute-start
  169.8 63.1 %reduce-scatter.25.cloned.1.call-start = ((), (), s32[]{:S(2)}) async-start(), calls=%async_computation.25 | async-start | bytes 1310720 | tf_op jit(solution)/shard_map/reduce_scatter | solution.py:36
  206.2 55.9 %all-gather.27.cloned.1.call-start = ((), (), s32[]{:S(2)}) async-start(), calls=%async_computation.26 | async-start | bytes 1310720 | tf_op jit(solution)/shard_map/all_gather | solution.py:32
  235.3 67.8 %reduce-scatter.27.cloned.1.call-start = ((), (), s32[]{:S(2)}) async-start(), calls=%async_computation.27 | async-start | bytes 1310720 | tf_op jit(solution)/shard_map/reduce_scatter | solution.py:36
  276.4 70.5 %all-gather.29.cloned.1.call-start = ((), (), s32[]{:S(2)}) async-start(), calls=%async_computation.28 | async-start | bytes 1310720 | tf_op jit(solution)/shard_map/all_gather | solution.py:32
  305.0 9.1 collective-permute-start.1
  319.0 63.7 %reduce-scatter.29.cloned.1.call-start = ((), (), s32[]{:S(2)}) async-start(), calls=%async_computation.29 | async-start | bytes 1310720 | tf_op jit(solution)/shard_map/reduce_scatter | solution.py:36
  355.9 56.5 %all-gather.31.cloned.1.call-start = ((), (), s32[]{:S(2)}) async-start(), calls=%async_computation.30 | async-start | bytes 1310720 | tf_op jit(solution)/shard_map/all_gather | solution.py:32
  385.6 67.8 %reduce-scatter.31.cloned.1.call-start = ((), (), s32[]{:S(2)}) async-start(), calls=%async_computation.31 | async-start | bytes 1310720 | tf_op jit(solution)/shard_map/reduce_scatter | solution.py:36
  426.7 70.6 %all-gather.33.cloned.1.call-start = ((), (), s32[]{:S(2)}) async-start(), calls=%async_computation.32 | async-start | bytes 1310720 | tf_op jit(solution)/shard_map/all_gather | solution.py:32
  455.4 9.1 collective-permute-start.2
  469.4 63.7 %reduce-scatter.33.cloned.1.call-start = ((), (), s32[]{:S(2)}) async-start(), calls=%async_computation.33 | async-start | bytes 1310720 | tf_op jit(solution)/shard_map/reduce_scatter | solution.py:36
  506.3 56.5 %all-gather.35.cloned.1.call-start = ((), (), s32[]{:S(2)}) async-start(), calls=%async_computation.34 | async-start | bytes 1310720 | tf_op jit(solution)/shard_map/all_gather | solution.py:32
  536.1 67.9 %reduce-scatter.35.cloned.1.call-start = ((), (), s32[]{:S(2)}) async-start(), calls=%async_computation.35 | async-start | bytes 1310720 | tf_op jit(solution)/shard_map/reduce_scatter | solution.py:36
  577.1 70.7 %all-gather.37.cloned.1.call-start = ((), (), s32[]{:S(2)}) async-start(), calls=%async_computation.36 | async-start | bytes 1310720 | tf_op jit(solution)/shard_map/all_gather | solution.py:32
  605.9 9.1 collective-permute-start.3
  619.9 63.7 %reduce-scatter.37.cloned.1.call-start = ((), (), s32[]{:S(2)}) async-start(), calls=%async_computation.37 | async-start | bytes 1310720 | tf_op jit(solution)/shard_map/reduce_scatter | solution.py:36
  656.9 56.5 %all-gather.39.cloned.1.call-start = ((), (), s32[]{:S(2)}) async-start(), calls=%async_computation.38 | async-start | bytes 1310720 | tf_op jit(solution)/shard_map/all_gather | solution.py:32
  686.6 55.7 %all-gather.41.cloned.1.call-start = ((), (), s32[]{:S(2)}) async-start(), calls=%async_computation.40 | async-start | bytes 1310720 | tf_op jit(solution)/shard_map/all_gather | solution.py:32
  689.0 96.1 %reduce-scatter.41.cloned.1.call-start = ((), (), s32[]{:S(2)}) async-start(), calls=%async_computation.41 | async-start | bytes 1310720 | tf_op jit(solution)/shard_map/reduce_scatter | solution.py:36
  758.3 61.6 %all-gather.43.cloned.1.call-start = ((), (), s32[]{:S(2)}) async-start(), calls=%async_computation.42 | async-start | bytes 1310720 | tf_op jit(solution)/shard_map/all_gather | solution.py:32
  793.1 74.4 %all-reduce.11.cloned.1.call-start = ((), (), s32[]{:S(2)}) async-start(), calls=%async_computation.44 | async-start | bytes 262144 | tf_op jit(solution)/shard_map/psum | solution.py:241
  833.4 63.7 %reduce-scatter.43.cloned.1.call-start = ((), (), s32[]{:S(2)}) async-start(), calls=%async_computation.43 | async-start | bytes 1310720 | tf_op jit(solution)/shard_map/reduce_scatter | solution.py:36
  836.8 102.5 %all-gather.45.cloned.1.call-start = ((), (), s32[]{:S(2)}) async-start(), calls=%async_computation.45 | async-start | bytes 1310720 | tf_op jit(solution)/shard_map/all_gather | solution.py:32
  901.4 10.1 collective-permute-start.4
  913.3 68.9 %reduce-scatter.45.cloned.1.call-start = ((), (), s32[]{:S(2)}) async-start(), calls=%async_computation.46 | async-start | bytes 1310720 | tf_op jit(solution)/shard_map/reduce_scatter | solution.py:36
  955.4 61.6 %all-gather.47.cloned.1.call-start = ((), (), s32[]{:S(2)}) async-start(), calls=%async_computation.47 | async-start | bytes 1310720 | tf_op jit(solution)/shard_map/all_gather | solution.py:32
  990.3 76.1 %all-reduce.13.cloned.1.call-start = ((), (), s32[]{:S(2)}) async-start(), calls=%async_computation.49 | async-start | bytes 262144 | tf_op jit(solution)/shard_map/psum | solution.py:241
  1032.3 63.8 %reduce-scatter.47.cloned.1.call-start = ((), (), s32[]{:S(2)}) async-start(), calls=%async_computation.48 | async-start | bytes 1310720 | tf_op jit(solution)/shard_map/reduce_scatter | solution.py:36
  1035.7 102.6 %all-gather.49.cloned.1.call-start = ((), (), s32[]{:S(2)}) async-start(), calls=%async_computation.50 | async-start | bytes 1310720 | tf_op jit(solution)/shard_map/all_gather | solution.py:32
  1100.4 10.1 collective-permute-start.5
  1112.3 68.9 %reduce-scatter.49.cloned.1.call-start = ((), (), s32[]{:S(2)}) async-start(), calls=%async_computation.51 | async-start | bytes 1310720 | tf_op jit(solution)/shard_map/reduce_scatter | solution.py:36
  1154.4 61.6 %all-gather.51.cloned.1.call-start = ((), (), s32[]{:S(2)}) async-start(), calls=%async_computation.52 | async-start | bytes 1310720 | tf_op jit(solution)/shard_map/all_gather | solution.py:32
  1189.3 76.1 %all-reduce.15.cloned.1.call-start = ((), (), s32[]{:S(2)}) async-start(), calls=%async_computation.54 | async-start | bytes 262144 | tf_op jit(solution)/shard_map/psum | solution.py:241
  1231.2 63.9 %reduce-scatter.51.cloned.1.call-start = ((), (), s32[]{:S(2)}) async-start(), calls=%async_computation.53 | async-start | bytes 1310720 | tf_op jit(solution)/shard_map/reduce_scatter | solution.py:36
  1234.7 102.7 %all-gather.53.cloned.1.call-start = ((), (), s32[]{:S(2)}) async-start(), calls=%async_computation.55 | async-start | bytes 1310720 | tf_op jit(solution)/shard_map/all_gather | solution.py:32
  1299.5 10.1 collective-permute-start.6
  1311.4 68.9 %reduce-scatter.53.cloned.1.call-start = ((), (), s32[]{:S(2)}) async-start(), calls=%async_computation.56 | async-start | bytes 1310720 | tf_op jit(solution)/shard_map/reduce_scatter | solution.py:36
  1353.5 61.6 %all-gather.55.cloned.1.call-start = ((), (), s32[]{:S(2)}) async-start(), calls=%async_computation.57 | async-start | bytes 1310720 | tf_op jit(solution)/shard_map/all_gather | solution.py:32
  1388.4 76.1 %all-reduce.17.cloned.1.call-start = ((), (), s32[]{:S(2)}) async-start(), calls=%async_computation.59 | async-start | bytes 262144 | tf_op jit(solution)/shard_map/psum | solution.py:241
  1430.4 63.6 %reduce-scatter.55.cloned.1.call-start = ((), (), s32[]{:S(2)}) async-start(), calls=%async_computation.58 | async-start | bytes 1310720 | tf_op jit(solution)/shard_map/reduce_scatter | solution.py:36
  1433.9 103.2 %all-gather.57.cloned.1.call-start = ((), (), s32[]{:S(2)}) async-start(), calls=%async_computation.60 | async-start | bytes 1310720 | tf_op jit(solution)/shard_map/all_gather | solution.py:32
  1498.3 9.9 collective-permute-start.7
  1511.1 68.9 %reduce-scatter.57.cloned.1.call-start = ((), (), s32[]{:S(2)}) async-start(), calls=%async_computation.61 | async-start | bytes 1310720 | tf_op jit(solution)/shard_map/reduce_scatter | solution.py:36
  1553.2 61.2 %all-gather.59.cloned.1.call-start = ((), (), s32[]{:S(2)}) async-start(), calls=%async_computation.62 | async-start | bytes 1310720 | tf_op jit(solution)/shard_map/all_gather | solution.py:32
  1587.6 228.8 %all-reduce.19.cloned.1.call-start = ((), (), s32[]{:S(2)}) async-start(), calls=%async_computation.64 | async-start | bytes 262144 | tf_op jit(solution)/shard_map/psum | solution.py:241
  1626.3 198.8 %reduce-scatter.39.cloned.1.call-start = ((), (), s32[]{:S(2)}) async-start(), calls=%async_computation.39 | async-start | bytes 1310720 | tf_op jit(solution)/shard_map/reduce_scatter | solution.py:36
  1636.0 211.8 %reduce-scatter.59.cloned.1.call-start = ((), (), s32[]{:S(2)}) async-start(), calls=%async_computation.63 | async-start | bytes 1310720 | tf_op jit(solution)/shard_map/reduce_scatter | solution.py:36
  1776.0 421.4 %all-reduce.21.cloned.1.call-start = ((), (), s32[]{:S(2)}) async-start(), calls=%async_computation.65 | async-start | bytes 44040192 | tf_op jit(solution)/shard_map/psum | solution.py:282
  1776.0 27.3 %copy-start.7 = (f32[2048,512]{1,0:T(8,128)S(1)}, f32[2048,512]{1,0:T(8,128)}, u32[]{:S(2)}) copy-start(f32[2048,512]{1,0:T(8,128)} %fusion.468) | copy-start | bytes 12582916
  1776.0 27.3 %copy-start.8 = (f32[2048,512]{1,0:T(8,128)S(1)}, f32[2048,512]{1,0:T(8,128)}, u32[]{:S(2)}) copy-start(f32[2048,512]{1,0:T(8,128)} %fusion.464) | copy-start | bytes 12582916
  1833.2 78.7 %copy-start.203 = (f32[64]{0:T(128)S(1)}, f32[64]{0:T(128)}, u32[]{:S(2)}) copy-start(f32[64]{0:T(128)} %copy-done.202) | copy-start | bytes 772
  1833.3 78.7 %copy-start.181 = (f32[64]{0:T(128)S(1)}, f32[64]{0:T(128)}, u32[]{:S(2)}) copy-start(f32[64]{0:T(128)} %copy-done.180) | copy-start | bytes 772
  1833.3 78.7 %copy-start.194 = (f32[64]{0:T(128)S(1)}, f32[64]{0:T(128)}, u32[]{:S(2)}) copy-start(f32[64]{0:T(128)} %fusion.724) | copy-start | bytes 772
  1850.4 63.1 %copy-start.39 = (f32[64,1,2048]{2,0,1:T(8,128)S(1)}, f32[64,1,2048]{2,0,1:T(8,128)}, u32[]{:S(2)}) copy-start(f32[64,1,2048]{2,0,1:T(8,128)} %copy-done.38) | copy-start | bytes 1572868
  (205 other events, 1062.7 us)
Sparse Core Ops, SparseCore 0:
  13.9 30.6 all-gather.20
  53.2 26.6 reduce-scatter.20
  85.3 26.5 all-gather.22
  127.2 26.6 reduce-scatter.22
  169.9 27.7 all-gather.24
  206.3 26.6 reduce-scatter.24
  235.5 26.5 all-gather.26
  276.5 26.6 reduce-scatter.26
  319.1 27.6 all-gather.28
  356.0 26.6 reduce-scatter.28
  385.8 26.5 all-gather.30
  426.8 26.5 reduce-scatter.30
  469.5 27.6 all-gather.32
  506.5 26.6 reduce-scatter.32
  536.2 26.5 all-gather.34
  577.2 26.6 reduce-scatter.34
  620.1 27.6 all-gather.36
  657.0 26.6 reduce-scatter.36
  686.7 26.5 all-gather.38
  714.8 27.4 all-gather.40
  758.5 26.6 reduce-scatter.40
  793.3 26.5 all-gather.42
  833.5 33.9 all-reduce.10
  870.3 26.7 reduce-scatter.42
  913.4 25.8 all-gather.44
  955.5 26.6 reduce-scatter.44
  990.4 26.5 all-gather.46
  1032.4 33.9 all-reduce.12
  1069.2 26.7 reduce-scatter.46
  1112.5 25.8 all-gather.48
  1154.5 26.6 reduce-scatter.48
  1189.4 26.5 all-gather.50
  1231.4 33.9 all-reduce.14
  1268.3 26.7 reduce-scatter.50
  1311.6 25.8 all-gather.52
  1353.6 26.6 reduce-scatter.52
  1388.5 26.5 all-gather.54
  1430.5 33.9 all-reduce.16
  1467.2 26.7 reduce-scatter.54
  1511.2 25.8 all-gather.56
  1553.3 26.6 reduce-scatter.56
  1587.7 26.5 all-gather.58
  1626.4 33.9 all-reduce.18
  1662.7 26.7 reduce-scatter.38
  1776.1 26.6 reduce-scatter.58
  1821.6 375.7 all-reduce.20
where the time goes:
time: 2250 us; the launch traced here: 2240 us
  waiting for transfers between devices  1340 us (60%)
  matrix products  463 us (21%)
  other arithmetic  188 us (8%)
  local copies, waits for them, and re-layouts  126 us (6%)
  blocking collectives  73 us (3%)
  starting transfers between devices  24.6 us (1%)
    all_gather x20, waiting for transfers between devices, gather_rows(): return lax.all_gather(own_rows, 'tensor', axis=0, tiled=True)  468 us
    reduce_scatter x20, waiting for transfers between devices, sum_rows(): lax.psum_scatter(term_fn(jnp.int32(0), own_count * lax.axis_size('tensor'...  462 us
    psum x1, waiting for transfers between devices, on_device(): lax.psum(for_sending(sharded_total), 'dp')  281 us
    psum x5, waiting for transfers between devices, on_device(): lax.psum(block_pairs.astype(jnp.bfloat16), 'tensor').astype(jnp.float32)  80.1 us
    dot_general x5, matrix products, on_device(): jnp.einsum('rsf,rsd->fd', active, grad_mlp, preferred_element_type=f32)  67.2 us
    dot_general x5, matrix products, on_device(): jnp.einsum('rsd,rsf->df', normed_two, grad_pre, preferred_element_type=f32)  66.3 us
    psum x1, blocking collectives, on_device(): common_total = lax.psum(common_total, ('tensor', 'dp'))  61.3 us
    ppermute x8, waiting for transfers between devices, from_behind(): return lax.ppermute(block, axis, route)  52.9 us
  transfers between devices with their start and end apart: 54, of which 51 were waited for; matrix products, arithmetic and copies ran while one was open for 16% of the time, Pallas kernels for 0%

commit v1 on v0

--- a/solution.py
+++ b/solution.py
@@ -7,6 +7,24 @@
 HD = 128
 
 
+def gather_around(array, axis, dim):
+    ways, here, step = (lax.axis_size(axis), lax.axis_index(axis), array.shape[dim])
+    shape = [n * ways if d == dim else n for d, n in enumerate(array.shape)]
+    full = lax.dynamic_update_slice_in_dim(
+        jnp.zeros(shape, array.dtype), array, here * step, axis=dim
+    )
+    going_up = going_down = array
+    for far in range(1, ways // 2 + 1):
+        going_up = lax.ppermute(going_up, axis, [(d, (d + 1) % ways) for d in range(ways)])
+        full = lax.dynamic_update_slice_in_dim(full, going_up, (here - far) % ways * step, axis=dim)
+        if 2 * far < ways:
+            going_down = lax.ppermute(going_down, axis, [(d, (d - 1) % ways) for d in range(ways)])
+            full = lax.dynamic_update_slice_in_dim(
+                full, going_down, (here + far) % ways * step, axis=dim
+            )
+    return full
+
+
 def from_behind(block, axis, distance):
     devices = range(lax.axis_size(axis))
     route = [(i - distance, i) for i in devices if i - distance in devices]
@@ -29,7 +47,7 @@
 
 
 def gather_rows(own_rows):
-    return lax.all_gather(own_rows, "tensor", axis=0, tiled=True)
+    return gather_around(own_rows, "tensor", 0)
 
 
 def sum_rows(term_fn, own_count):

time: 2250 us -> 2070 us (0.920)
  waiting for transfers between devices: 1340 us -> 1090 us
  starting transfers between devices: 24.6 us -> 104 us
  local copies, waits for them, and re-layouts: 126 us -> 155 us
  matrix products: 463 us -> 439 us
    all_gather x20 -> x0, waiting for transfers between devices: 468 us -> none  [gather_rows(): return lax.all_gather(own_rows, 'tensor', axis=0, tiled=True)]
    ppermute x0 -> x60, waiting for transfers between devices: none -> 297 us  [the longest x40 233 us: gather_around(): lax.ppermute(going_up, axis, [(d, (d + 1) % ways) for d in range(ways)])]
    ppermute x0 -> x60, starting transfers between devices: none -> 82.6 us  [the longest x20 74.4 us: gather_around(): lax.ppermute(going_down, axis, [(d, (d - 1) % ways) for d in range(ways)])]
    reduce_scatter x20, waiting for transfers between devices: 462 us -> 392 us  [sum_rows(): lax.psum_scatter(term_fn(jnp.int32(0), own_count * lax.axis_size('tensor'...]
    convert_element_type x18 -> x0, other arithmetic: 23.6 us -> none  [the longest x5 9.11 us: on_device(): layer_norm(layer_input, gain_one, bias_one).astype(bf16)]
  transfers between devices with their start and end apart: 54 -> 94, of which waited for: 51 -> 90; matrix products, arithmetic and copies ran while one was open for 16% -> 18% of each run, Pallas kernels for 0% -> 0%
where the time goes in v1:
time: 2070 us; the launch traced here: 2060 us
  waiting for transfers between devices  1090 us (53%)
  matrix products  439 us (21%)
  other arithmetic  177 us (9%)
  local copies, waits for them, and re-layouts  155 us (7%)
  starting transfers between devices  104 us (5%)
  blocking collectives  71.4 us (3%)
    reduce_scatter x20, waiting for transfers between devices, sum_rows(): lax.psum_scatter(term_fn(jnp.int32(0), own_count * lax.axis_size('tensor'...  392 us
    psum x1, waiting for transfers between devices, on_device(): lax.psum(for_sending(sharded_total), 'dp')  281 us
    ppermute x40, waiting for transfers between devices, gather_around(): lax.ppermute(going_up, axis, [(d, (d + 1) % ways) for d in range(ways)])  233 us
    psum x5, waiting for transfers between devices, on_device(): lax.psum(block_pairs.astype(jnp.bfloat16), 'tensor').astype(jnp.float32)  76 us
    ppermute x20, starting transfers between devices, gather_around(): lax.ppermute(going_down, axis, [(d, (d - 1) % ways) for d in range(ways)])  74.4 us
    dot_general x5, matrix products, on_device(): jnp.einsum('rsf,rsd->fd', active, grad_mlp, preferred_element_type=f32)  67.6 us
    dot_general x5, matrix products, on_device(): jnp.einsum('rsd,rsf->df', normed_two, grad_pre, preferred_element_type=f32)  66.3 us
    ppermute x20, waiting for transfers between devices, gather_around(): lax.ppermute(going_down, axis, [(d, (d - 1) % ways) for d in range(ways)])  64.3 us
  transfers between devices with their start and end apart: 94, of which 90 were waited for; matrix products, arithmetic and copies ran while one was open for 18% of the time, Pallas kernels for 0%

profile of v1, /device:TPU:0, one launch (start us, length us, event | category | flops | bytes accessed | tf_op | source)
XLA Modules:
  0.0 2059.7 jit_solution(6091803770521869871)
XLA Ops:
  19.1 7.3 collective-permute-done
  47.3 26.5 %reduce-scatter.21.cloned.1.call-done = bf16[64,1,2048]{2,0,1:T(8,128)(2,1)} async-done(((bf16[256,1,2048]{2,0,1:T(8,128)(2,1)}), bf16[64,1,2048]{2,0,1:T(8,128)(2,1)}) %reduce-scatter.21.cloned.1.call-update) | async-done | bytes 262160 | tf_op jit(solution)/shard_map/reduce_scatter | solution.py:54
  82.3 7.2 collective-permute-done.3
  92.1 7.4 collective-permute-done.5
  104.0 7.2 bitcast_dynamic-update-slice_fusion.4
  114.9 25.3 %reduce-scatter.23.cloned.1.call-done = bf16[64,1,2048]{2,0,1:T(8,128)(2,1)} async-done(((bf16[256,1,2048]{2,0,1:T(8,128)(2,1)}), bf16[64,1,2048]{2,0,1:T(8,128)(2,1)}) %reduce-scatter.23.cloned.1.call-update) | async-done | bytes 262160 | tf_op jit(solution)/shard_map/reduce_scatter | solution.py:54
  161.2 7.4 collective-permute-done.7
  188.0 26.4 %reduce-scatter.25.cloned.1.call-done = bf16[64,1,2048]{2,0,1:T(8,128)(2,1)} async-done(((bf16[256,1,2048]{2,0,1:T(8,128)(2,1)}), bf16[64,1,2048]{2,0,1:T(8,128)(2,1)}) %reduce-scatter.25.cloned.1.call-update) | async-done | bytes 262160 | tf_op jit(solution)/shard_map/reduce_scatter | solution.py:54
  220.1 7.2 collective-permute-done.10
  229.9 7.4 collective-permute-done.12
  237.3 7.5 bitcast_dynamic-update-slice_fusion.3
  248.4 25.4 %reduce-scatter.27.cloned.1.call-done = bf16[64,1,2048]{2,0,1:T(8,128)(2,1)} async-done(((bf16[256,1,2048]{2,0,1:T(8,128)(2,1)}), bf16[64,1,2048]{2,0,1:T(8,128)(2,1)}) %reduce-scatter.27.cloned.1.call-update) | async-done | bytes 262160 | tf_op jit(solution)/shard_map/reduce_scatter | solution.py:54
  294.6 7.5 collective-permute-done.14
  322.1 26.3 %reduce-scatter.29.cloned.1.call-done = bf16[64,1,2048]{2,0,1:T(8,128)(2,1)} async-done(((bf16[256,1,2048]{2,0,1:T(8,128)(2,1)}), bf16[64,1,2048]{2,0,1:T(8,128)(2,1)}) %reduce-scatter.29.cloned.1.call-update) | async-done | bytes 262160 | tf_op jit(solution)/shard_map/reduce_scatter | solution.py:54
  354.1 7.2 collective-permute-done.17
  363.9 7.4 collective-permute-done.19
  371.3 7.5 bitcast_dynamic-update-slice_fusion.2
  382.4 25.4 %reduce-scatter.31.cloned.1.call-done = bf16[64,1,2048]{2,0,1:T(8,128)(2,1)} async-done(((bf16[256,1,2048]{2,0,1:T(8,128)(2,1)}), bf16[64,1,2048]{2,0,1:T(8,128)(2,1)}) %reduce-scatter.31.cloned.1.call-update) | async-done | bytes 262160 | tf_op jit(solution)/shard_map/reduce_scatter | solution.py:54
  428.8 7.5 collective-permute-done.21
  456.4 26.3 %reduce-scatter.33.cloned.1.call-done = bf16[64,1,2048]{2,0,1:T(8,128)(2,1)} async-done(((bf16[256,1,2048]{2,0,1:T(8,128)(2,1)}), bf16[64,1,2048]{2,0,1:T(8,128)(2,1)}) %reduce-scatter.33.cloned.1.call-update) | async-done | bytes 262160 | tf_op jit(solution)/shard_map/reduce_scatter | solution.py:54
  488.4 7.2 collective-permute-done.24
  498.1 7.4 collective-permute-done.26
  505.6 7.5 bitcast_dynamic-update-slice_fusion.1
  546.4 9.8 reduce-scatter.35.cloned.1.call-done
  574.2 7.0 collective-permute-done.28
  583.7 7.1 collective-permute-done.30
  610.9 14.3 reduce-scatter.37.cloned.1.call-done
  651.0 8.1 bitcast_dynamic-update-slice_fusion
  659.0 8.4 convert_reduce_fusion.4
  690.7 9.9 reduce-scatter.41.cloned.1.call-done
  760.6 15.3 all-reduce.11.cloned.1.call-done
  776.8 28.7 %reduce-scatter.43.cloned.1.call-done = bf16[64,1,2048]{2,0,1:T(8,128)(2,1)} async-done(((bf16[256,1,2048]{2,0,1:T(8,128)(2,1)}), bf16[64,1,2048]{2,0,1:T(8,128)(2,1)}) %reduce-scatter.43.cloned.1.call-update) | async-done | bytes 262160 | tf_op jit(solution)/shard_map/reduce_scatter | solution.py:54
  811.0 8.8 collective-permute-done.40
  825.0 7.2 collective-permute-done.41
  841.2 8.5 convert_reduce_fusion.3
  859.2 22.9 %reduce-scatter.45.cloned.1.call-done = bf16[64,1,2048]{2,0,1:T(8,128)(2,1)} async-done(((bf16[256,1,2048]{2,0,1:T(8,128)(2,1)}), bf16[64,1,2048]{2,0,1:T(8,128)(2,1)}) %reduce-scatter.45.cloned.1.call-update) | async-done | bytes 262160 | tf_op jit(solution)/shard_map/reduce_scatter | solution.py:54
  938.5 19.8 all-reduce.13.cloned.1.call-done
  959.9 27.9 %reduce-scatter.47.cloned.1.call-done = bf16[64,1,2048]{2,0,1:T(8,128)(2,1)} async-done(((bf16[256,1,2048]{2,0,1:T(8,128)(2,1)}), bf16[64,1,2048]{2,0,1:T(8,128)(2,1)}) %reduce-scatter.47.cloned.1.call-update) | async-done | bytes 262160 | tf_op jit(solution)/shard_map/reduce_scatter | solution.py:54
  993.5 8.8 collective-permute-done.47
  1007.4 7.2 collective-permute-done.48
  1023.7 8.6 convert_reduce_fusion.2
  1041.8 22.7 %reduce-scatter.49.cloned.1.call-done = bf16[64,1,2048]{2,0,1:T(8,128)(2,1)} async-done(((bf16[256,1,2048]{2,0,1:T(8,128)(2,1)}), bf16[64,1,2048]{2,0,1:T(8,128)(2,1)}) %reduce-scatter.49.cloned.1.call-update) | async-done | bytes 262160 | tf_op jit(solution)/shard_map/reduce_scatter | solution.py:54
  1120.7 20.1 all-reduce.15.cloned.1.call-done
  1142.4 28.1 %reduce-scatter.51.cloned.1.call-done = bf16[64,1,2048]{2,0,1:T(8,128)(2,1)} async-done(((bf16[256,1,2048]{2,0,1:T(8,128)(2,1)}), bf16[64,1,2048]{2,0,1:T(8,128)(2,1)}) %reduce-scatter.51.cloned.1.call-update) | async-done | bytes 262160 | tf_op jit(solution)/shard_map/reduce_scatter | solution.py:54
  1225.4 15.8 reduce-scatter.53.cloned.1.call-done
  1296.7 20.8 %all-reduce.17.cloned.1.call-done = bf16[256,1,256]{0,2,1:T(8,128)(2,1)} async-done(((bf16[256,1,256]{0,2,1:T(8,128)(2,1)}), bf16[256,1,256]{0,2,1:T(8,128)(2,1)}) %all-reduce.17.cloned.1.call-update) | async-done | bytes 131088 | tf_op jit(solution)/shard_map/psum | solution.py:259
  1319.0 28.1 %reduce-scatter.55.cloned.1.call-done = bf16[64,1,2048]{2,0,1:T(8,128)(2,1)} async-done(((bf16[256,1,2048]{2,0,1:T(8,128)(2,1)}), bf16[64,1,2048]{2,0,1:T(8,128)(2,1)}) %reduce-scatter.55.cloned.1.call-update) | async-done | bytes 262160 | tf_op jit(solution)/shard_map/reduce_scatter | solution.py:54
  1354.2 7.4 collective-permute-done.61
  1383.0 8.6 convert_reduce_fusion
  1400.9 10.4 fusion.447
  1460.2 9.7 fusion.456
  1479.7 9.5 fusion.454
  1489.3 10.0 fusion.445
  1508.9 9.9 fusion.452
  1518.8 10.4 fusion.443
  1538.8 9.9 fusion.450
  1548.7 10.1 fusion.441
  1569.9 26.7 %fusion = bf16[1,2048,2048]{2,1,0:T(8,128)(2,1)} fusion(f32[2048,2048]{1,0:T(8,128)} %fusion.441, f32[2048,2048]{1,0:T(8,128)} %fusion.443, f32[2048,2048]{1,0:T(8,128)} %fusion.447, f32[2048,2048]{1,0:T(8,128)} %fusion.445, bf16[256,2048]{1,0:T(8,128)(2,1)S(1)} %copy-done.55, f32[4,256,1,2048]{3,1,2,0:T(8,128)} %get-tuple-element.244, s32[]{:T(128)S(6)} %select_n.587), kind=kOutput, calls=%fused_computation.2 | convolution fusion | flops 2173173760 | bytes 78643200 | tf_op jit(solution)/shard_map/rsf,rsd->fd/dot_general | solution.py:208
  1600.4 27.3 %fusion.41 = bf16[1,2048,2048]{2,1,0:T(8,128)(2,1)} fusion(bf16[256,2048]{1,0:T(8,128)(2,1)} %copy-done.122, f32[2048,2048]{1,0:T(8,128)} %fusion.450, f32[2048,2048]{1,0:T(8,128)} %fusion.452, f32[2048,2048]{1,0:T(8,128)} %fusion.456, f32[2048,2048]{1,0:T(8,128)} %fusion.454, bf16[4,256,1,2048]{3,1,2,0:T(8,128)(2,1)} %bitcast_dynamic-update-slice_fusion.5, ...), kind=kOutput, calls=%fused_computation.43 | convolution fusion | flops 2168455168 | bytes 77594624 | tf_op jit(solution)/shard_map/rsd,rsf->df/dot_general | solution.py:209
  1659.7 11.2 all-reduce.2
  1675.3 60.3 %all-reduce.1 = (f32[1,2048]{1,0:T(1,128)}, f32[1,2048]{1,0:T(1,128)}, f32[1,2048]{1,0:T(1,128)}, f32[1,2048]{1,0:T(1,128)}, f32[1,2048]{1,0:T(1,128)}, /*index=5*/f32[1,2048]{1,0:T(1,128)}) all-reduce(f32[1,2048]{1,0:T(1,128)S(1)} %bitcast.1447, ...), channel_id=1, replica_groups=mesh['section'=2,'tensor'=4,'dp'=4] {'tensor','dp'}, use_global_device_ids=true, to_apply=%region_105.106 | all-reduce | flops 12288 | bytes 98304 | tf_op jit(solution)/shard_map/psum | solution.py:302
  1739.9 280.6 %all-reduce.21.cloned.1.call-done = (bf16[1,2048,512]{2,1,0:T(8,128)(2,1)}, bf16[1,2048,256]{2,1,0:T(8,128)(2,1)}, bf16[1,512,2048]{2,1,0:T(8,128)(2,1)}, bf16[1...) async-done(((bf16[1,2048,512]{2,1,0:T(8,128)(2,1)}, bf16[1,2048,256]{2,1,0:T(8,128)(2,1)}, bf16[1,512,2048]{2,1,0:T(8,128)(2,1)}, bf16[1,2048,2048]{2,1,0:T(8,128)(2,1)}, ...) | async-done | bytes 22020112 | tf_op jit(solution)/shard_map/psum | solution.py:300
  2029.6 11.7 broadcast_in_dim.547
  2041.3 11.7 broadcast_in_dim.551
  (1113 shorter events, 853.4 us)
Async XLA Ops:
  7.2 66.5 %reduce-scatter.21.cloned.1.call-start = ((), (), s32[]{:S(2)}) async-start(), calls=%async_computation.20 | async-start | bytes 1310720 | tf_op jit(solution)/shard_map/reduce_scatter | solution.py:54
  13.9 12.4 collective-permute-start
  16.9 13.9 collective-permute-start.1
  47.1 93.1 %reduce-scatter.23.cloned.1.call-start = ((), (), s32[]{:S(2)}) async-start(), calls=%async_computation.21 | async-start | bytes 1310720 | tf_op jit(solution)/shard_map/reduce_scatter | solution.py:54
  78.5 13.6 collective-permute-start.4
  114.8 99.6 %reduce-scatter.25.cloned.1.call-start = ((), (), s32[]{:S(2)}) async-start(), calls=%async_computation.22 | async-start | bytes 1310720 | tf_op jit(solution)/shard_map/reduce_scatter | solution.py:54
  157.3 11.3 collective-permute-start.7
  157.3 13.3 collective-permute-start.8
  188.0 85.8 %reduce-scatter.27.cloned.1.call-start = ((), (), s32[]{:S(2)}) async-start(), calls=%async_computation.23 | async-start | bytes 1310720 | tf_op jit(solution)/shard_map/reduce_scatter | solution.py:54
  216.3 13.5 collective-permute-start.11
  248.3 100.2 %reduce-scatter.29.cloned.1.call-start = ((), (), s32[]{:S(2)}) async-start(), calls=%async_computation.24 | async-start | bytes 1310720 | tf_op jit(solution)/shard_map/reduce_scatter | solution.py:54
  290.7 11.4 collective-permute-start.14
  290.7 13.6 collective-permute-start.15
  322.1 85.7 %reduce-scatter.31.cloned.1.call-start = ((), (), s32[]{:S(2)}) async-start(), calls=%async_computation.25 | async-start | bytes 1310720 | tf_op jit(solution)/shard_map/reduce_scatter | solution.py:54
  350.3 11.1 collective-permute-start.17
  350.3 13.6 collective-permute-start.18
  382.4 100.3 %reduce-scatter.33.cloned.1.call-start = ((), (), s32[]{:S(2)}) async-start(), calls=%async_computation.26 | async-start | bytes 1310720 | tf_op jit(solution)/shard_map/reduce_scatter | solution.py:54
  425.0 11.4 collective-permute-start.21
  425.0 13.5 collective-permute-start.22
  456.3 99.8 %reduce-scatter.35.cloned.1.call-start = ((), (), s32[]{:S(2)}) async-start(), calls=%async_computation.27 | async-start | bytes 1310720 | tf_op jit(solution)/shard_map/reduce_scatter | solution.py:54
  484.5 11.1 collective-permute-start.24
  484.6 13.6 collective-permute-start.25
  516.6 108.5 %reduce-scatter.37.cloned.1.call-start = ((), (), s32[]{:S(2)}) async-start(), calls=%async_computation.28 | async-start | bytes 1310720 | tf_op jit(solution)/shard_map/reduce_scatter | solution.py:54
  519.0 16.9 collective-permute-start.34
  519.0 24.8 %collective-permute-start.35 = (bf16[64,1,2048]{2,0,1:T(8,128)(2,1)}, bf16[64,1,2048]{2,0,1:T(8,128)(2,1)}, u32[]{:S(2)}, u32[]{:S(2)}) collective-permute-start(bf16[64,1,2048]{2,0,1:T(8,128)(2,1)} %get-tuple-element.203), channel_id=1, source_target_pairs={{0,12},{4,0},{8,4},{12,8},{1,13},{5,1},{9,5},{13,9},{2,14},{6,2},{... | collective-permute-start | bytes 786440 | tf_op jit(solution)/shard_map/ppermute | solution.py:21
  535.9 25.7 %collective-permute-start.36 = (bf16[64,1,2048]{2,0,1:T(8,128)(2,1)}, bf16[64,1,2048]{2,0,1:T(8,128)(2,1)}, u32[]{:S(2)}, u32[]{:S(2)}) collective-permute-start(bf16[64,1,2048]{2,0,1:T(8,128)(2,1)} %collective-permute-done.34), channel_id=1, source_target_pairs={{0,4},{4,8},{8,12},{12,0},{1,5},{5,9},{9,13},{13,1},{2,6},{6,10},{... | collective-permute-start | bytes 786440 | tf_op jit(solution)/shard_map/ppermute | solution.py:18
  569.8 11.5 collective-permute-start.28
  570.3 13.4 collective-permute-start.29
  598.7 101.9 %reduce-scatter.41.cloned.1.call-start = ((), (), s32[]{:S(2)}) async-start(), calls=%async_computation.30 | async-start | bytes 1310720 | tf_op jit(solution)/shard_map/reduce_scatter | solution.py:54
  629.1 11.4 collective-permute-start.31
  630.4 14.5 collective-permute-start.32
  675.2 100.7 %all-reduce.11.cloned.1.call-start = ((), (), s32[]{:S(2)}) async-start(), calls=%async_computation.32 | async-start | bytes 262144 | tf_op jit(solution)/shard_map/psum | solution.py:259
  707.9 11.3 collective-permute-start.37
  711.0 13.8 collective-permute-start.38
  743.1 62.4 %reduce-scatter.43.cloned.1.call-start = ((), (), s32[]{:S(2)}) async-start(), calls=%async_computation.31 | async-start | bytes 1310720 | tf_op jit(solution)/shard_map/reduce_scatter | solution.py:54
  746.6 135.5 %reduce-scatter.45.cloned.1.call-start = ((), (), s32[]{:S(2)}) async-start(), calls=%async_computation.33 | async-start | bytes 1310720 | tf_op jit(solution)/shard_map/reduce_scatter | solution.py:54
  821.1 11.1 collective-permute-start.41
  821.1 13.1 collective-permute-start.42
  857.5 100.8 %all-reduce.13.cloned.1.call-start = ((), (), s32[]{:S(2)}) async-start(), calls=%async_computation.35 | async-start | bytes 262144 | tf_op jit(solution)/shard_map/psum | solution.py:259
  889.5 11.1 collective-permute-start.44
  892.3 13.8 collective-permute-start.45
  925.5 62.4 %reduce-scatter.47.cloned.1.call-start = ((), (), s32[]{:S(2)}) async-start(), calls=%async_computation.34 | async-start | bytes 1310720 | tf_op jit(solution)/shard_map/reduce_scatter | solution.py:54
  929.0 135.5 %reduce-scatter.49.cloned.1.call-start = ((), (), s32[]{:S(2)}) async-start(), calls=%async_computation.36 | async-start | bytes 1310720 | tf_op jit(solution)/shard_map/reduce_scatter | solution.py:54
  1003.5 11.1 collective-permute-start.48
  1003.6 13.1 collective-permute-start.49
  1040.0 100.8 %all-reduce.15.cloned.1.call-start = ((), (), s32[]{:S(2)}) async-start(), calls=%async_computation.38 | async-start | bytes 262144 | tf_op jit(solution)/shard_map/psum | solution.py:259
  1071.9 11.1 collective-permute-start.51
  1074.7 13.8 collective-permute-start.52
  1108.0 62.4 %reduce-scatter.51.cloned.1.call-start = ((), (), s32[]{:S(2)}) async-start(), calls=%async_computation.37 | async-start | bytes 1310720 | tf_op jit(solution)/shard_map/reduce_scatter | solution.py:54
  1111.5 129.8 %reduce-scatter.53.cloned.1.call-start = ((), (), s32[]{:S(2)}) async-start(), calls=%async_computation.39 | async-start | bytes 1310720 | tf_op jit(solution)/shard_map/reduce_scatter | solution.py:54
  1189.7 12.5 collective-permute-start.56
  1216.5 100.9 %all-reduce.17.cloned.1.call-start = ((), (), s32[]{:S(2)}) async-start(), calls=%async_computation.41 | async-start | bytes 262144 | tf_op jit(solution)/shard_map/psum | solution.py:259
  1248.7 11.1 collective-permute-start.58
  1251.5 13.8 collective-permute-start.59
  1284.7 62.5 %reduce-scatter.55.cloned.1.call-start = ((), (), s32[]{:S(2)}) async-start(), calls=%async_computation.40 | async-start | bytes 1310720 | tf_op jit(solution)/shard_map/reduce_scatter | solution.py:54
  1288.2 132.3 %reduce-scatter.57.cloned.1.call-start = ((), (), s32[]{:S(2)}) async-start(), calls=%async_computation.42 | async-start | bytes 1310720 | tf_op jit(solution)/shard_map/reduce_scatter | solution.py:54
  1362.9 11.1 collective-permute-start.62
  1364.0 14.1 collective-permute-start.63
  1396.0 244.9 %all-reduce.19.cloned.1.call-start = ((), (), s32[]{:S(2)}) async-start(), calls=%async_computation.44 | async-start | bytes 262144 | tf_op jit(solution)/shard_map/psum | solution.py:259
  1427.4 11.1 collective-permute-start.65
  1428.6 14.1 collective-permute-start.66
  1460.1 187.6 %reduce-scatter.39.cloned.1.call-start = ((), (), s32[]{:S(2)}) async-start(), calls=%async_computation.29 | async-start | bytes 1310720 | tf_op jit(solution)/shard_map/reduce_scatter | solution.py:54
  1469.9 202.6 %reduce-scatter.59.cloned.1.call-start = ((), (), s32[]{:S(2)}) async-start(), calls=%async_computation.43 | async-start | bytes 1310720 | tf_op jit(solution)/shard_map/reduce_scatter | solution.py:54
  1599.9 420.5 %all-reduce.21.cloned.1.call-start = ((), (), s32[]{:S(2)}) async-start(), calls=%async_computation.45 | async-start | bytes 44040192 | tf_op jit(solution)/shard_map/psum | solution.py:300
  (279 other events, 3916.2 us)
Sparse Core Ops, SparseCore 0:
  47.2 26.4 reduce-scatter.20
  114.9 25.2 reduce-scatter.22
  188.1 26.2 reduce-scatter.24
  248.4 25.3 reduce-scatter.26
  322.2 26.2 reduce-scatter.28
  382.5 25.2 reduce-scatter.30
  456.5 26.1 reduce-scatter.32
  516.7 39.3 reduce-scatter.34
  598.8 26.2 reduce-scatter.36
  675.3 25.2 reduce-scatter.40
  743.2 32.6 all-reduce.10
  778.7 26.7 reduce-scatter.42
  857.6 24.3 reduce-scatter.44
  925.6 32.6 all-reduce.12
  961.0 26.7 reduce-scatter.46
  1040.1 24.3 reduce-scatter.48
  1108.1 32.6 all-reduce.14
  1143.6 26.7 reduce-scatter.50
  1216.6 24.5 reduce-scatter.52
  1284.8 32.6 all-reduce.16
  1320.3 26.8 reduce-scatter.54
  1396.1 24.3 reduce-scatter.56
  1460.3 32.5 all-reduce.18
  1495.1 26.7 reduce-scatter.38
  1600.1 25.2 reduce-scatter.58
  1646.0 374.4 all-reduce.20
